TPU v7x, 32 devices: a whole 2x2x4 slice. The times are simulated.
32 devices in a mesh: shard: 4 (over z), tensor: 2 (over core), section: 4 (over y, x).
Axes of the slice: x: 2, y: 2, z: 4, core: 2. Of those that a mesh axis runs over, the one named last changes fastest.
Arguments:
- gradient: bfloat16 [2560, 2560], P('shard', ('tensor', 'section')), may hold values from -100 to 100
- gain_grad: float32 [2, 2560], P(None, 'shard'), may hold values from -12 to 12
- left_statistic: float32 [2560, 2560], P('shard', ('tensor', 'section')), may hold values from -1 to 3, as said below
- left_basis: float32 [2560, 2560], P('shard', ('tensor', 'section')), may hold values from -1 to 1.5
- first_moment: float32 [2560, 2560], P('shard', ('tensor', 'section')), may hold values from -3 to 3
- second_moment: float32 [2560, 2560], P('shard', ('tensor', 'section')), may hold values from 0.2 to 2
- norm_gains: float32 [2, 2560], P(None, 'shard'), may hold values from 0.5 to 1.5
- gain_first: float32 [2, 2560], P(None, 'shard'), may hold values from -2 to 2
- gain_second: float32 [2, 2560], P(None, 'shard'), may hold values from 0.5 to 5
Outputs:
- update: float32 [2560, 2560], P('shard', ('tensor', 'section'))
- new_first: float32 [2560, 2560], P('shard', ('tensor', 'section'))
- new_second: float32 [2560, 2560], P('shard', ('tensor', 'section'))
- new_statistic: float32 [2560, 2560], P('shard', ('tensor', 'section'))
- new_basis: float32 [2560, 2560], P('shard', ('tensor', 'section'))
- new_gains: float32 [2, 2560], P(None, 'shard')
- new_gain_first: float32 [2, 2560], P(None, 'shard')
- new_gain_second: float32 [2, 2560], P(None, 'shard')
Inputs may be any that keep to these rules, and one draw needn't show every extreme that they name: `left_statistic`: symmetric.
All inputs are finite; a program needn't handle non-finite values.
Results may differ from a plain program's by a relative error of at most 0.0003.
Values may be sent and summed in bfloat16 or wider, within the bound.
A program may use at most 128 MiB of HBM per device.

v0:
```python
import jax
import jax.numpy as jnp
from jax import lax
from jax.sharding import PartitionSpec as P

D = 2560
NS_STEPS = 3
GROUP = ("tensor", "section")
EVERY = ("shard", "tensor", "section")
PAD = 16


def matmul(left_side, right_side):
    return jnp.dot(
        left_side, right_side, precision=lax.Precision.HIGH, preferred_element_type=jnp.float32
    )


def row_panel(local_block):
    return lax.all_gather(local_block, GROUP, axis=1, tiled=True)


def same(block):
    return block


def pack(block):
    top = jnp.max(jnp.abs(block), axis=0, keepdims=True)
    power = jnp.clip(jnp.ceil(jnp.log2(jnp.maximum(top, 1e-30))) - 14.0, -110.0, 120.0)
    scaled = block * jnp.exp2(-power)
    tail = jnp.broadcast_to(power, (PAD, block.shape[1]))
    return jnp.concatenate([scaled, tail], axis=0).astype(jnp.float16)


def unpack(payload):
    values = payload.astype(jnp.float32)
    return values[..., :-PAD, :] * jnp.exp2(values[..., -PAD : -PAD + 1, :])


def partners(size):
    if size & size - 1 == 0:
        return [[(one, one ^ offset) for one in range(size)] for offset in range(1, size)]
    return [[(one, (one + offset) % size) for one in range(size)] for offset in range(1, size)]


def place_of_source(place, offset, size):
    return place ^ offset if size & size - 1 == 0 else (place - offset) % size


def place_of_target(place, offset, size):
    return place ^ offset if size & size - 1 == 0 else (place + offset) % size


def shard_total(value, shards):
    if shards > 8:
        return lax.psum(value, "shard")
    tile = jnp.full((8, 128), value, jnp.float32)
    total = value
    for pairs in partners(shards):
        total = total + lax.ppermute(tile, "shard", pairs)[0, 0]
    return total


def rows_times_shards(full_rows, block, shards, place, encode, decode):
    if shards > 8:
        gathered = decode(lax.all_gather(encode(block), "shard", axis=0))
        return matmul(full_rows, gathered.reshape(-1, block.shape[1]))
    rows = block.shape[0]
    sent = encode(block)
    pieces = [block] + [decode(lax.ppermute(sent, "shard", pairs)) for pairs in partners(shards)]
    total = None
    for offset, piece in enumerate(pieces):
        source = place_of_source(place, offset, shards)
        left = lax.dynamic_slice_in_dim(full_rows, source * rows, rows, 1)
        term = matmul(left, piece)
        total = term if total is None else total + term
    return total


def scatter_product(full_rows, block, shards, place, encode, decode):
    if shards > 8:
        return lax.psum_scatter(
            matmul(full_rows.T, block), "shard", scatter_dimension=0, tiled=True
        )
    rows = full_rows.shape[1] // shards
    arrived = []
    for offset, pairs in enumerate(partners(shards), 1):
        target = place_of_target(place, offset, shards)
        chunk = matmul(lax.dynamic_slice_in_dim(full_rows, target * rows, rows, 1).T, block)
        arrived.append(lax.ppermute(encode(chunk), "shard", pairs))
    total = matmul(lax.dynamic_slice_in_dim(full_rows, place * rows, rows, 1).T, block)
    for payload in arrived:
        total = total + decode(payload)
    return total


def outer_block(gradient, grad_rows, shards, group, place, member):
    rows, cols = gradient.shape
    if rows % cols == 0 and shards <= 8:
        own = lax.dynamic_slice_in_dim(grad_rows, member * cols % rows, cols, 0)
        other = jnp.zeros_like(own)
        for offset in range(1, shards):
            pairs = []
            for column in range(group):
                home = column * cols // rows
                pairs.append((home * group + column, (home + offset) % shards * group + column))
            other = other + lax.ppermute(own, EVERY, pairs)
        partner = jnp.where(place == member * cols // rows, own, other)
        return jnp.dot(grad_rows, partner.T, preferred_element_type=jnp.float32)
    partner = lax.all_gather(gradient, "shard", axis=0, tiled=True)
    product = jnp.dot(gradient, partner.T, preferred_element_type=jnp.float32)
    return lax.psum_scatter(product, GROUP, scatter_dimension=1, tiled=True)


def on_device(
    gradient,
    gain_grad,
    left_statistic,
    left_basis,
    first_moment,
    second_moment,
    norm_gains,
    gain_first,
    gain_second,
):
    group = lax.axis_size(GROUP)
    shards = lax.axis_size("shard")
    place = lax.axis_index("shard")
    member = lax.axis_index(GROUP)
    rows, cols = gradient.shape
    grad_float = gradient.astype(jnp.float32)
    grad_rows = row_panel(gradient)
    late_basis, grad_rows = lax.optimization_barrier((left_basis, grad_rows))
    basis_rows = row_panel(late_basis)
    grad_rows_float = grad_rows.astype(jnp.float32)
    squares_total = shard_total(
        jnp.sum(grad_rows_float * grad_rows_float) + jnp.sum(gain_grad * gain_grad), shards
    )
    clip_factor = jnp.minimum(1.0, D / jnp.sqrt(squares_total + 1e-06))
    outer_part = outer_block(gradient, grad_rows, shards, group, place, member)
    new_statistic = 0.95 * left_statistic + 0.05 / D * clip_factor * clip_factor * outer_part
    ready_statistic, basis_rows = lax.optimization_barrier((new_statistic, basis_rows))
    statistic_rows = row_panel(ready_statistic)
    power_product = rows_times_shards(statistic_rows, left_basis, shards, place, same, same)
    power_rows = row_panel(power_product)
    rotated = clip_factor * scatter_product(basis_rows, grad_float, shards, place, same, same)
    new_first = 0.9 * first_moment + 0.1 * rotated
    new_second = 0.95 * second_moment + 0.05 * rotated * rotated
    direction = new_first / (jnp.sqrt(new_second) + 1e-08)
    update = rows_times_shards(
        basis_rows,
        direction,
        shards,
        place,
        lambda x: x.astype(jnp.float16),
        lambda x: x.astype(jnp.float32),
    )
    update, power_rows = lax.optimization_barrier((update, power_rows))
    power_sum = shard_total(jnp.sum(power_rows * power_rows), shards)
    scale = 0.9 * jnp.sqrt(D / (power_sum + 1e-06))
    iterate = scale * power_product
    iterate_rows = scale * power_rows
    row_index = place * rows + lax.broadcasted_iota(jnp.int32, (rows, cols), 0)
    col_index = member * cols + lax.broadcasted_iota(jnp.int32, (rows, cols), 1)
    eye = (row_index == col_index).astype(jnp.float32)
    for sweep_index in range(NS_STEPS):
        if sweep_index:
            iterate_rows = row_panel(iterate)
            gram_block = scatter_product(iterate_rows, iterate, shards, place, pack, unpack)
        else:
            gram_block = (
                scale
                * scale
                * scatter_product(power_rows, power_product, shards, place, pack, unpack)
            )
        iterate = iterate - 0.5 * rows_times_shards(
            iterate_rows, gram_block - eye, shards, place, pack, unpack
        )
    gain_clipped = clip_factor * gain_grad
    new_gain_first = 0.9 * gain_first + 0.1 * gain_clipped
    new_gain_second = 0.95 * gain_second + 0.05 * gain_clipped * gain_clipped
    new_gains = norm_gains - 0.01 * new_gain_first / (jnp.sqrt(new_gain_second) + 1e-08)
    return (
        update,
        new_first,
        new_second,
        new_statistic,
        iterate,
        new_gains,
        new_gain_first,
        new_gain_second,
    )


def solution(mesh):
    matrix = P("shard", GROUP)
    vector = P(None, "shard")
    return jax.shard_map(
        on_device,
        mesh=mesh,
        in_specs=(matrix, vector, matrix, matrix, matrix, matrix, vector, vector, vector),
        out_specs=(matrix, matrix, matrix, matrix, matrix, vector, vector, vector),
        check_vma=False,
    )
```

profile of v0, /device:TPU:8, one launch (start us, length us, event | category | flops | bytes accessed | tf_op | source)
XLA Modules:
  0.0 734.5 jit_solution(14928106622082852291)
XLA Ops:
  7.9 36.0 %all-gather.7.cloned.1.call-done = bf16[640,2560]{0,1:T(8,128)(2,1)} async-done(((bf16[640,320]{0,1:T(8,128)(2,1)}), bf16[640,2560]{0,1:T(8,128)(2,1)}) %all-gather.7.cloned.1.call-update) | async-done | bytes 3276816 | tf_op jit(solution)/shard_map/all_gather | solution.py:20
  44.0 4.1 constant_dynamic-slice_fusion
  48.1 4.1 copy.18
  61.4 5.8 collective-permute-start
  67.2 43.5 %collective-permute-done = f32[8,128]{1,0:T(8,128)S(1)} collective-permute-done((f32[8,128]{1,0:T(8,128)S(1)}, f32[8,128]{1,0:T(8,128)S(1)}, u32[]{:S(2)}, u32[]{:S(2)}) %collective-permute-start) | collective-permute-done | bytes 4128 | tf_op jit(solution)/shard_map/ppermute | solution.py:60
  115.5 3.9 copy.20
  119.4 3.9 copy.21
  123.2 3.8 copy.23
  127.1 5.5 fusion.152
  133.5 3.6 collective-permute-start.13
  137.0 40.8 %all-gather.11.cloned.1.call-done = f32[640,2560]{0,1:T(8,128)} async-done(((f32[640,320]{0,1:T(8,128)}), f32[640,2560]{0,1:T(8,128)}) %all-gather.11.cloned.1.call-update) | async-done | bytes 6553616 | tf_op jit(solution)/shard_map/all_gather | solution.py:20
  202.0 29.3 %collective-permute-done.6 = f32[640,320]{0,1:T(8,128)S(1)} collective-permute-done((f32[640,320]{0,1:T(8,128)S(1)}, f32[640,320]{0,1:T(8,128)S(1)}, u32[]{:S(2)}, u32[]{:S(2)}) %collective-permute-start.6) | collective-permute-done | bytes 819232 | tf_op jit(solution)/shard_map/ppermute | solution.py:90
  231.3 23.9 %collective-permute-done.7 = f32[640,320]{0,1:T(8,128)S(1)} collective-permute-done((f32[640,320]{0,1:T(8,128)S(1)}, f32[640,320]{0,1:T(8,128)S(1)}, u32[]{:S(2)}, u32[]{:S(2)}) %collective-permute-start.7) | collective-permute-done | bytes 819232 | tf_op jit(solution)/shard_map/ppermute | solution.py:90
  255.2 16.5 %collective-permute-done.8 = f32[640,320]{0,1:T(8,128)S(1)} collective-permute-done((f32[640,320]{0,1:T(8,128)S(1)}, f32[640,320]{0,1:T(8,128)S(1)}, u32[]{:S(2)}, u32[]{:S(2)}) %collective-permute-start.8) | collective-permute-done | bytes 819232 | tf_op jit(solution)/shard_map/ppermute | solution.py:90
  280.4 21.3 %collective-permute-done.10 = f16[640,320]{0,1:T(8,128)(2,1)S(1)} collective-permute-done((f16[640,320]{0,1:T(8,128)(2,1)S(1)}, f16[640,320]{0,1:T(8,128)(2,1)S(1)}, u32[]{:S(2)}, u32[]{:S(2)}) %collective-permute-start.10) | collective-permute-done | bytes 409632 | tf_op jit(solution)/shard_map/ppermute | solution.py:70
  303.0 7.1 collective-permute-done.11
  331.4 24.1 %collective-permute-done.15 = f32[8,128]{1,0:T(8,128)S(1)} collective-permute-done((f32[8,128]{1,0:T(8,128)S(1)}, f32[8,128]{1,0:T(8,128)S(1)}, u32[]{:S(2)}, u32[]{:S(2)}) %collective-permute-start.15) | collective-permute-done | bytes 4128 | tf_op jit(solution)/shard_map/ppermute | solution.py:60
  357.3 7.6 %collective-permute-done.16 = f32[8,128]{1,0:T(8,128)S(1)} collective-permute-done((f32[8,128]{1,0:T(8,128)S(1)}, f32[8,128]{1,0:T(8,128)S(1)}, u32[]{:S(2)}, u32[]{:S(2)}) %collective-permute-start.16) | collective-permute-done | bytes 4128 | tf_op jit(solution)/shard_map/ppermute | solution.py:60
  381.2 25.5 %collective-permute-done.22 = f16[656,320]{0,1:T(8,128)(2,1)S(1)} collective-permute-done((f16[656,320]{0,1:T(8,128)(2,1)S(1)}, f16[656,320]{0,1:T(8,128)(2,1)S(1)}, u32[]{:S(2)}, u32[]{:S(2)}) %collective-permute-start.22) | collective-permute-done | bytes 419872 | tf_op jit(solution)/shard_map/ppermute | solution.py:70
  408.2 10.3 %collective-permute-done.23 = f16[656,320]{0,1:T(8,128)(2,1)S(1)} collective-permute-done((f16[656,320]{0,1:T(8,128)(2,1)S(1)}, f16[656,320]{0,1:T(8,128)(2,1)S(1)}, u32[]{:S(2)}, u32[]{:S(2)}) %collective-permute-start.23) | collective-permute-done | bytes 419872 | tf_op jit(solution)/shard_map/ppermute | solution.py:70
  423.0 46.7 %all-gather.15.cloned.1.call-done = f32[640,2560]{0,1:T(8,128)} async-done(((f32[640,320]{0,1:T(8,128)}), f32[640,2560]{0,1:T(8,128)}) %all-gather.15.cloned.1.call-update) | async-done | bytes 6553616 | tf_op jit(solution)/shard_map/all_gather | solution.py:20
  482.2 9.0 %collective-permute-done.24 = f16[656,320]{0,1:T(8,128)(2,1)S(1)} collective-permute-done((f16[656,320]{0,1:T(8,128)(2,1)S(1)}, f16[656,320]{0,1:T(8,128)(2,1)S(1)}, u32[]{:S(2)}, u32[]{:S(2)}) %collective-permute-start.24) | collective-permute-done | bytes 419872 | tf_op jit(solution)/shard_map/ppermute | solution.py:90
  491.2 21.4 %collective-permute-done.25 = f16[656,320]{0,1:T(8,128)(2,1)S(1)} collective-permute-done((f16[656,320]{0,1:T(8,128)(2,1)S(1)}, f16[656,320]{0,1:T(8,128)(2,1)S(1)}, u32[]{:S(2)}, u32[]{:S(2)}) %collective-permute-start.25) | collective-permute-done | bytes 419872 | tf_op jit(solution)/shard_map/ppermute | solution.py:90
  513.0 10.2 %collective-permute-done.26 = f16[656,320]{0,1:T(8,128)(2,1)S(1)} collective-permute-done((f16[656,320]{0,1:T(8,128)(2,1)S(1)}, f16[656,320]{0,1:T(8,128)(2,1)S(1)}, u32[]{:S(2)}, u32[]{:S(2)}) %collective-permute-start.26) | collective-permute-done | bytes 419872 | tf_op jit(solution)/shard_map/ppermute | solution.py:90
  531.5 27.0 %collective-permute-done.28 = f16[656,320]{0,1:T(8,128)(2,1)S(1)} collective-permute-done((f16[656,320]{0,1:T(8,128)(2,1)S(1)}, f16[656,320]{0,1:T(8,128)(2,1)S(1)}, u32[]{:S(2)}, u32[]{:S(2)}) %collective-permute-start.28) | collective-permute-done | bytes 419872 | tf_op jit(solution)/shard_map/ppermute | solution.py:70
  558.6 11.4 %collective-permute-done.29 = f16[656,320]{0,1:T(8,128)(2,1)S(1)} collective-permute-done((f16[656,320]{0,1:T(8,128)(2,1)S(1)}, f16[656,320]{0,1:T(8,128)(2,1)S(1)}, u32[]{:S(2)}, u32[]{:S(2)}) %collective-permute-start.29) | collective-permute-done | bytes 419872 | tf_op jit(solution)/shard_map/ppermute | solution.py:70
  575.9 44.9 %all-gather.17.cloned.1.call-done = f32[640,2560]{0,1:T(8,128)} async-done(((f32[640,320]{0,1:T(8,128)}), f32[640,2560]{0,1:T(8,128)}) %all-gather.17.cloned.1.call-update) | async-done | bytes 6553616 | tf_op jit(solution)/shard_map/all_gather | solution.py:20
  633.4 9.0 %collective-permute-done.30 = f16[656,320]{0,1:T(8,128)(2,1)S(1)} collective-permute-done((f16[656,320]{0,1:T(8,128)(2,1)S(1)}, f16[656,320]{0,1:T(8,128)(2,1)S(1)}, u32[]{:S(2)}, u32[]{:S(2)}) %collective-permute-start.30) | collective-permute-done | bytes 419872 | tf_op jit(solution)/shard_map/ppermute | solution.py:90
  642.5 21.4 %collective-permute-done.31 = f16[656,320]{0,1:T(8,128)(2,1)S(1)} collective-permute-done((f16[656,320]{0,1:T(8,128)(2,1)S(1)}, f16[656,320]{0,1:T(8,128)(2,1)S(1)}, u32[]{:S(2)}, u32[]{:S(2)}) %collective-permute-start.31) | collective-permute-done | bytes 419872 | tf_op jit(solution)/shard_map/ppermute | solution.py:90
  664.3 10.2 %collective-permute-done.32 = f16[656,320]{0,1:T(8,128)(2,1)S(1)} collective-permute-done((f16[656,320]{0,1:T(8,128)(2,1)S(1)}, f16[656,320]{0,1:T(8,128)(2,1)S(1)}, u32[]{:S(2)}, u32[]{:S(2)}) %collective-permute-start.32) | collective-permute-done | bytes 419872 | tf_op jit(solution)/shard_map/ppermute | solution.py:90
  683.4 26.4 %collective-permute-done.34 = f16[656,320]{0,1:T(8,128)(2,1)S(1)} collective-permute-done((f16[656,320]{0,1:T(8,128)(2,1)S(1)}, f16[656,320]{0,1:T(8,128)(2,1)S(1)}, u32[]{:S(2)}, u32[]{:S(2)}) %collective-permute-start.34) | collective-permute-done | bytes 419872 | tf_op jit(solution)/shard_map/ppermute | solution.py:70
  709.9 11.4 %collective-permute-done.35 = f16[656,320]{0,1:T(8,128)(2,1)S(1)} collective-permute-done((f16[656,320]{0,1:T(8,128)(2,1)S(1)}, f16[656,320]{0,1:T(8,128)(2,1)S(1)}, u32[]{:S(2)}, u32[]{:S(2)}) %collective-permute-start.35) | collective-permute-done | bytes 419872 | tf_op jit(solution)/shard_map/ppermute | solution.py:70
  (243 shorter events, 143.6 us)
Async XLA Ops:
  7.2 36.8 %all-gather.7.cloned.1.call-start = ((), (), s32[]{:S(2)}) async-start(), calls=%async_computation | async-start | bytes 3686400 | tf_op jit(solution)/shard_map/all_gather | solution.py:20
  7.9 124.7 %all-gather.9.cloned.1.call-start = ((), (), s32[]{:S(2)}) async-start(), calls=%async_computation.1 | async-start | bytes 7372800 | tf_op jit(solution)/shard_map/all_gather | solution.py:20
  44.0 133.9 %all-gather.11.cloned.1.call-start = ((), (), s32[]{:S(2)}) async-start(), calls=%async_computation.2 | async-start | bytes 7372800 | tf_op jit(solution)/shard_map/all_gather | solution.py:20
  52.2 63.3 %collective-permute-start.3 = (bf16[320,2560]{1,0:T(8,128)(2,1)}, bf16[320,2560]{1,0:T(8,128)(2,1)}, u32[]{:S(2)}, u32[]{:S(2)}) collective-permute-start(bf16[320,2560]{1,0:T(8,128)(2,1)} %copy.18), channel_id=1, source_target_pairs={{0,8},{1,9},{10,18},{11,19},{20,28},{21,29},{30,6},{31,7}} | collective-permute-start | bytes 4915208 | tf_op jit(solution)/shard_map/ppermute | solution.py:107
  53.5 65.9 %collective-permute-start.4 = (bf16[320,2560]{1,0:T(8,128)(2,1)}, bf16[320,2560]{1,0:T(8,128)(2,1)}, u32[]{:S(2)}, u32[]{:S(2)}) collective-permute-start(bf16[320,2560]{1,0:T(8,128)(2,1)} %copy.18), channel_id=1, source_target_pairs={{0,16},{1,17},{10,26},{11,27},{20,4},{21,5},{30,14},{31,15}} | collective-permute-start | bytes 4915208 | tf_op jit(solution)/shard_map/ppermute | solution.py:107
  55.4 67.9 %collective-permute-start.5 = (bf16[320,2560]{1,0:T(8,128)(2,1)}, bf16[320,2560]{1,0:T(8,128)(2,1)}, u32[]{:S(2)}, u32[]{:S(2)}) collective-permute-start(bf16[320,2560]{1,0:T(8,128)(2,1)} %copy.18), channel_id=1, source_target_pairs={{0,24},{1,25},{10,2},{11,3},{20,12},{21,13},{30,22},{31,23}} | collective-permute-start | bytes 4915208 | tf_op jit(solution)/shard_map/ppermute | solution.py:107
  61.4 49.3 %collective-permute-start = (f32[8,128]{1,0:T(8,128)S(1)}, f32[8,128]{1,0:T(8,128)S(1)}, u32[]{:S(2)}, u32[]{:S(2)}) collective-permute-start(f32[8,128]{1,0:T(8,128)S(1)} %broadcast_in_dim.28), channel_id=1, source_target_pairs={{0,8},{8,0},{16,24},{24,16},{1,9},{9,1},{17,25},{25,17},{2,10},{10... | collective-permute-start | bytes 12296 | tf_op jit(solution)/shard_map/ppermute | solution.py:60
  67.2 44.7 %collective-permute-start.1 = (f32[8,128]{1,0:T(8,128)S(1)}, f32[8,128]{1,0:T(8,128)S(1)}, u32[]{:S(2)}, u32[]{:S(2)}) collective-permute-start(f32[8,128]{1,0:T(8,128)S(1)} %broadcast_in_dim.28), channel_id=1, source_target_pairs={{0,16},{8,24},{16,0},{24,8},{1,17},{9,25},{17,1},{25,9},{2,18},{10... | collective-permute-start | bytes 12296 | tf_op jit(solution)/shard_map/ppermute | solution.py:60
  132.6 181.2 %all-gather.13.cloned.1.call-start = ((), (), s32[]{:S(2)}) async-start(), calls=%async_computation.3 | async-start | bytes 7372800 | tf_op jit(solution)/shard_map/all_gather | solution.py:20
  132.6 48.3 %collective-permute-start.14 = (f32[640,320]{0,1:T(8,128)}, f32[640,320]{0,1:T(8,128)S(1)}, u32[]{:S(2)}, u32[]{:S(2)}) collective-permute-start(f32[640,320]{0,1:T(8,128)} %param.12), channel_id=1, source_target_pairs={{0,24},{8,16},{16,8},{24,0},{1,25},{9,17},{17,9},{25,1},{2,26},{10... | collective-permute-start | bytes 2457608 | tf_op jit(solution)/shard_map/ppermute | solution.py:70
  133.5 53.0 %collective-permute-start.13 = (f32[640,320]{0,1:T(8,128)}, f32[640,320]{0,1:T(8,128)S(1)}, u32[]{:S(2)}, u32[]{:S(2)}) collective-permute-start(f32[640,320]{0,1:T(8,128)} %param.12), channel_id=1, source_target_pairs={{0,16},{8,24},{16,0},{24,8},{1,17},{9,25},{17,1},{25,9},{2,18},{10... | collective-permute-start | bytes 2457608 | tf_op jit(solution)/shard_map/ppermute | solution.py:70
  137.0 50.8 %collective-permute-start.12 = (f32[640,320]{0,1:T(8,128)}, f32[640,320]{0,1:T(8,128)S(1)}, u32[]{:S(2)}, u32[]{:S(2)}) collective-permute-start(f32[640,320]{0,1:T(8,128)} %param.12), channel_id=1, source_target_pairs={{0,8},{8,0},{16,24},{24,16},{1,9},{9,1},{17,25},{25,17},{2,10},{10... | collective-permute-start | bytes 2457608 | tf_op jit(solution)/shard_map/ppermute | solution.py:70
  190.1 279.5 %all-gather.15.cloned.1.call-start = ((), (), s32[]{:S(2)}) async-start(), calls=%async_computation.4 | async-start | bytes 7372800 | tf_op jit(solution)/shard_map/all_gather | solution.py:20
  200.4 54.8 %collective-permute-start.7 = (f32[640,320]{0,1:T(8,128)S(1)}, f32[640,320]{0,1:T(8,128)S(1)}, u32[]{:S(2)}, u32[]{:S(2)}) collective-permute-start(f32[640,320]{0,1:T(8,128)S(1)} %fusion.67), channel_id=1, source_target_pairs={{0,16},{8,24},{16,0},{24,8},{1,17},{9,25},{17,1},{25,9},{2,18},{10... | collective-permute-start | bytes 2457608 | tf_op jit(solution)/shard_map/ppermute | solution.py:90
  201.4 70.3 %collective-permute-start.8 = (f32[640,320]{0,1:T(8,128)S(1)}, f32[640,320]{0,1:T(8,128)S(1)}, u32[]{:S(2)}, u32[]{:S(2)}) collective-permute-start(f32[640,320]{0,1:T(8,128)S(1)} %fusion.63), channel_id=1, source_target_pairs={{0,24},{8,16},{16,8},{24,0},{1,25},{9,17},{17,9},{25,1},{2,26},{10... | collective-permute-start | bytes 2457608 | tf_op jit(solution)/shard_map/ppermute | solution.py:90
  274.6 35.6 %collective-permute-start.11 = (f16[640,320]{0,1:T(8,128)(2,1)S(1)}, f16[640,320]{0,1:T(8,128)(2,1)S(1)}, u32[]{:S(2)}, u32[]{:S(2)}) collective-permute-start(f16[640,320]{0,1:T(8,128)(2,1)S(1)} %get-tuple-element.23), channel_id=1, source_target_pairs={{0,24},{8,16},{16,8},{24,0},{1,25},{9,17},{17,9},{25,1},{2,26},{10... | collective-permute-start | bytes 1228808 | tf_op jit(solution)/shard_map/ppermute | solution.py:70
  276.2 35.3 %collective-permute-start.9 = (f16[640,320]{0,1:T(8,128)(2,1)S(1)}, f16[640,320]{0,1:T(8,128)(2,1)S(1)}, u32[]{:S(2)}, u32[]{:S(2)}) collective-permute-start(f16[640,320]{0,1:T(8,128)(2,1)S(1)} %get-tuple-element.23), channel_id=1, source_target_pairs={{0,8},{8,0},{16,24},{24,16},{1,9},{9,1},{17,25},{25,17},{2,10},{10... | collective-permute-start | bytes 1228808 | tf_op jit(solution)/shard_map/ppermute | solution.py:70
  322.0 47.1 %collective-permute-start.18 = (f16[656,320]{0,1:T(8,128)(2,1)S(1)}, f16[656,320]{0,1:T(8,128)(2,1)S(1)}, u32[]{:S(2)}, u32[]{:S(2)}) collective-permute-start(f16[656,320]{0,1:T(8,128)(2,1)S(1)} %pad_maximum_fusion), channel_id=1, source_target_pairs={{0,8},{8,0},{16,24},{24,16},{1,9},{9,1},{17,25},{25,17},{2,10},{10... | collective-permute-start | bytes 1259528 | tf_op jit(solution)/shard_map/ppermute | solution.py:90
  322.5 46.7 %collective-permute-start.19 = (f16[656,320]{0,1:T(8,128)(2,1)S(1)}, f16[656,320]{0,1:T(8,128)(2,1)S(1)}, u32[]{:S(2)}, u32[]{:S(2)}) collective-permute-start(f16[656,320]{0,1:T(8,128)(2,1)S(1)} %pad_maximum_fusion.1), channel_id=1, source_target_pairs={{0,16},{8,24},{16,0},{24,8},{1,17},{9,25},{17,1},{25,9},{2,18},{10... | collective-permute-start | bytes 1259528 | tf_op jit(solution)/shard_map/ppermute | solution.py:90
  324.8 44.8 %collective-permute-start.20 = (f16[656,320]{0,1:T(8,128)(2,1)S(1)}, f16[656,320]{0,1:T(8,128)(2,1)}, u32[]{:S(2)}, u32[]{:S(2)}) collective-permute-start(f16[656,320]{0,1:T(8,128)(2,1)S(1)} %pad_maximum_fusion.2), channel_id=1, source_target_pairs={{0,24},{8,16},{16,8},{24,0},{1,25},{9,17},{17,9},{25,1},{2,26},{10... | collective-permute-start | bytes 1259528 | tf_op jit(solution)/shard_map/ppermute | solution.py:90
  330.5 34.4 %collective-permute-start.16 = (f32[8,128]{1,0:T(8,128)S(1)}, f32[8,128]{1,0:T(8,128)S(1)}, u32[]{:S(2)}, u32[]{:S(2)}) collective-permute-start(f32[8,128]{1,0:T(8,128)S(1)} %broadcast_in_dim.29), channel_id=1, source_target_pairs={{0,16},{8,24},{16,0},{24,8},{1,17},{9,25},{17,1},{25,9},{2,18},{10... | collective-permute-start | bytes 12296 | tf_op jit(solution)/shard_map/ppermute | solution.py:60
  376.9 41.6 %collective-permute-start.23 = (f16[656,320]{0,1:T(8,128)(2,1)S(1)}, f16[656,320]{0,1:T(8,128)(2,1)S(1)}, u32[]{:S(2)}, u32[]{:S(2)}) collective-permute-start(f16[656,320]{0,1:T(8,128)(2,1)S(1)} %pad_maximum_fusion.3), channel_id=1, source_target_pairs={{0,24},{8,16},{16,8},{24,0},{1,25},{9,17},{17,9},{25,1},{2,26},{10... | collective-permute-start | bytes 1259528 | tf_op jit(solution)/shard_map/ppermute | solution.py:70
  379.5 40.6 %collective-permute-start.21 = (f16[656,320]{0,1:T(8,128)(2,1)S(1)}, f16[656,320]{0,1:T(8,128)(2,1)S(1)}, u32[]{:S(2)}, u32[]{:S(2)}) collective-permute-start(f16[656,320]{0,1:T(8,128)(2,1)S(1)} %pad_maximum_fusion.3), channel_id=1, source_target_pairs={{0,8},{8,0},{16,24},{24,16},{1,9},{9,1},{17,25},{25,17},{2,10},{10... | collective-permute-start | bytes 1259528 | tf_op jit(solution)/shard_map/ppermute | solution.py:70
  422.9 198.0 %all-gather.17.cloned.1.call-start = ((), (), s32[]{:S(2)}) async-start(), calls=%async_computation.5 | async-start | bytes 7372800 | tf_op jit(solution)/shard_map/all_gather | solution.py:20
  477.5 35.2 %collective-permute-start.25 = (f16[656,320]{0,1:T(8,128)(2,1)S(1)}, f16[656,320]{0,1:T(8,128)(2,1)S(1)}, u32[]{:S(2)}, u32[]{:S(2)}) collective-permute-start(f16[656,320]{0,1:T(8,128)(2,1)S(1)} %pad_maximum_fusion.5), channel_id=1, source_target_pairs={{0,16},{8,24},{16,0},{24,8},{1,17},{9,25},{17,1},{25,9},{2,18},{10... | collective-permute-start | bytes 1259528 | tf_op jit(solution)/shard_map/ppermute | solution.py:90
  481.9 41.4 %collective-permute-start.26 = (f16[656,320]{0,1:T(8,128)(2,1)S(1)}, f16[656,320]{0,1:T(8,128)(2,1)S(1)}, u32[]{:S(2)}, u32[]{:S(2)}) collective-permute-start(f16[656,320]{0,1:T(8,128)(2,1)S(1)} %pad_maximum_fusion.6), channel_id=1, source_target_pairs={{0,24},{8,16},{16,8},{24,0},{1,25},{9,17},{17,9},{25,1},{2,26},{10... | collective-permute-start | bytes 1259528 | tf_op jit(solution)/shard_map/ppermute | solution.py:90
  525.8 44.2 %collective-permute-start.29 = (f16[656,320]{0,1:T(8,128)(2,1)S(1)}, f16[656,320]{0,1:T(8,128)(2,1)S(1)}, u32[]{:S(2)}, u32[]{:S(2)}) collective-permute-start(f16[656,320]{0,1:T(8,128)(2,1)S(1)} %pad_maximum_fusion.7), channel_id=1, source_target_pairs={{0,24},{8,16},{16,8},{24,0},{1,25},{9,17},{17,9},{25,1},{2,26},{10... | collective-permute-start | bytes 1259528 | tf_op jit(solution)/shard_map/ppermute | solution.py:70
  527.6 42.8 %collective-permute-start.27 = (f16[656,320]{0,1:T(8,128)(2,1)S(1)}, f16[656,320]{0,1:T(8,128)(2,1)S(1)}, u32[]{:S(2)}, u32[]{:S(2)}) collective-permute-start(f16[656,320]{0,1:T(8,128)(2,1)S(1)} %pad_maximum_fusion.7), channel_id=1, source_target_pairs={{0,8},{8,0},{16,24},{24,16},{1,9},{9,1},{17,25},{25,17},{2,10},{10... | collective-permute-start | bytes 1259528 | tf_op jit(solution)/shard_map/ppermute | solution.py:70
  628.8 35.2 %collective-permute-start.31 = (f16[656,320]{0,1:T(8,128)(2,1)S(1)}, f16[656,320]{0,1:T(8,128)(2,1)S(1)}, u32[]{:S(2)}, u32[]{:S(2)}) collective-permute-start(f16[656,320]{0,1:T(8,128)(2,1)S(1)} %pad_maximum_fusion.9), channel_id=1, source_target_pairs={{0,16},{8,24},{16,0},{24,8},{1,17},{9,25},{17,1},{25,9},{2,18},{10... | collective-permute-start | bytes 1259528 | tf_op jit(solution)/shard_map/ppermute | solution.py:90
  633.1 41.4 %collective-permute-start.32 = (f16[656,320]{0,1:T(8,128)(2,1)S(1)}, f16[656,320]{0,1:T(8,128)(2,1)S(1)}, u32[]{:S(2)}, u32[]{:S(2)}) collective-permute-start(f16[656,320]{0,1:T(8,128)(2,1)S(1)} %pad_maximum_fusion.10), channel_id=1, source_target_pairs={{0,24},{8,16},{16,8},{24,0},{1,25},{9,17},{17,9},{25,1},{2,26},{10... | collective-permute-start | bytes 1259528 | tf_op jit(solution)/shard_map/ppermute | solution.py:90
  677.1 44.2 %collective-permute-start.35 = (f16[656,320]{0,1:T(8,128)(2,1)S(1)}, f16[656,320]{0,1:T(8,128)(2,1)S(1)}, u32[]{:S(2)}, u32[]{:S(2)}) collective-permute-start(f16[656,320]{0,1:T(8,128)(2,1)S(1)} %pad_maximum_fusion.11), channel_id=1, source_target_pairs={{0,24},{8,16},{16,8},{24,0},{1,25},{9,17},{17,9},{25,1},{2,26},{10... | collective-permute-start | bytes 1259528 | tf_op jit(solution)/shard_map/ppermute | solution.py:70
  679.5 42.2 %collective-permute-start.33 = (f16[656,320]{0,1:T(8,128)(2,1)S(1)}, f16[656,320]{0,1:T(8,128)(2,1)S(1)}, u32[]{:S(2)}, u32[]{:S(2)}) collective-permute-start(f16[656,320]{0,1:T(8,128)(2,1)S(1)} %pad_maximum_fusion.11), channel_id=1, source_target_pairs={{0,8},{8,0},{16,24},{24,16},{1,9},{9,1},{17,25},{25,17},{2,10},{10... | collective-permute-start | bytes 1259528 | tf_op jit(solution)/shard_map/ppermute | solution.py:70
  (31 other events, 647.4 us)
Sparse Core Ops, SparseCore 0:
  9.9 34.0 all-gather.6
  45.8 46.6 all-gather.8
  132.7 45.0 all-gather.10
  190.2 47.2 all-gather.12
  423.0 46.5 all-gather.14
  576.1 44.7 all-gather.16
where the time goes:
time: 743 us; the launch traced here: 734 us
  waiting for transfers between devices  542 us (73%)
  matrix products  81.2 us (11%)
  starting transfers between devices  49.9 us (7%)
  local copies, waits for them, and re-layouts  25 us (3%)
  between operations  21.4 us (3%)
  other arithmetic  15.3 us (2%)
    all_gather x6, waiting for transfers between devices, row_panel(): return lax.all_gather(local_block, GROUP, axis=1, tiled=True)  168 us
    ppermute x12, waiting for transfers between devices, scatter_product(): arrived.append(lax.ppermute(encode(chunk), 'shard', pairs))  151 us
    ppermute x15, waiting for transfers between devices, rows_times_shards(): lax.ppermute(sent, 'shard', pairs)  143 us
    ppermute x6, waiting for transfers between devices, shard_total(): total = total + lax.ppermute(tile, 'shard', pairs)[0, 0]  78.2 us
    dot_general x36, matrix products, matmul(): jnp.dot(left_side, right_side, precision=lax.Precision.HIGH, preferred_el...  75.7 us
    ppermute x15, starting transfers between devices, rows_times_shards(): lax.ppermute(sent, 'shard', pairs)  22.2 us
  transfers between devices with their start and end apart: 42, of which 27 were waited for; matrix products, arithmetic and copies ran while one was open for 11% of the time, Pallas kernels for 0%

commit v1 on v0

--- a/solution.py
+++ b/solution.py
@@ -17,7 +17,36 @@
 
 
 def row_panel(local_block):
-    return lax.all_gather(local_block, GROUP, axis=1, tiled=True)
+
+    def plan_sections(slab_in):
+        kept_arr, placed, main = (
+            jax.lax.axis_size(GROUP),
+            jax.lax.axis_index(GROUP),
+            slab_in.shape[1],
+        )
+        grid = tuple(((s, (s + 1) % kept_arr) for s in range(kept_arr)))
+        steps_seen = tuple(((s, (s - 1) % kept_arr) for s in range(kept_arr)))
+        everything = jnp.zeros(
+            (*slab_in.shape[:1], kept_arr * main, *slab_in.shape[2:]), slab_in.dtype
+        )
+        everything = lax.dynamic_update_slice_in_dim(everything, slab_in, placed * main, axis=1)
+        long_array = oldest = slab_in
+        before = kept_arr // 2
+        ii = 1
+        while ii < before + 1:
+            long_array = jax.lax.ppermute(long_array, GROUP, grid)
+            everything = lax.dynamic_update_slice_in_dim(
+                everything, long_array, (placed - ii) % kept_arr * main, axis=1
+            )
+            if ii < kept_arr - before:
+                oldest = jax.lax.ppermute(oldest, GROUP, steps_seen)
+                everything = lax.dynamic_update_slice_in_dim(
+                    everything, oldest, (placed + ii) % kept_arr * main, axis=1
+                )
+            ii += 1
+        return everything
+
+    return plan_sections(local_block)
 
 
 def same(block):

time: 743 us -> 1110 us (1.49)
  waiting for transfers between devices: 542 us -> 814 us
  local copies, waits for them, and re-layouts: 25 us -> 88.5 us
  starting transfers between devices: 49.9 us -> 96.5 us
  between operations: 21.4 us -> 8.29 us
    ppermute x0 -> x42, waiting for transfers between devices: none -> 505 us  [the longest x24 315 us: plan_sections(): long_array = jax.lax.ppermute(long_array, GROUP, grid)]
    all_gather x6 -> x0, waiting for transfers between devices: 168 us -> none  [row_panel(): return lax.all_gather(local_block, GROUP, axis=1, tiled=True)]
    dynamic_update_slice x0 -> x45, local copies, waits for them, and re-layouts: none -> 73.8 us  [the longest x24 36.9 us: plan_sections(): lax.dynamic_update_slice_in_dim(everything, long_array, (placed - ii) % k...]
    ppermute x0 -> x42, starting transfers between devices: none -> 53 us  [the longest x18 27.7 us: plan_sections(): oldest = jax.lax.ppermute(oldest, GROUP, steps_seen)]
    ppermute x6, waiting for transfers between devices: 78.2 us -> 35.3 us  [shard_total(): total = total + lax.ppermute(tile, 'shard', pairs)[0, 0]]
    ppermute x12, waiting for transfers between devices: 151 us -> 136 us  [scatter_product(): arrived.append(lax.ppermute(encode(chunk), 'shard', pairs))]
    ppermute x3 -> x0, local copies, waits for them, and re-layouts: 11.6 us -> none  [outer_block(): other = other + lax.ppermute(own, EVERY, pairs)]
  transfers between devices with their start and end apart: 42 -> 78, of which waited for: 27 -> 59; matrix products, arithmetic and copies ran while one was open for 11% -> 12% of each run, Pallas kernels for 0% -> 0%
where the time goes in v1:
time: 1110 us; the launch traced here: 1100 us
  waiting for transfers between devices  814 us (73%)
  starting transfers between devices  96.5 us (9%)
  local copies, waits for them, and re-layouts  88.5 us (8%)
  matrix products  72.4 us (7%)
  other arithmetic  19.1 us (2%)
    ppermute x24, waiting for transfers between devices, plan_sections(): long_array = jax.lax.ppermute(long_array, GROUP, grid)  315 us
    ppermute x18, waiting for transfers between devices, plan_sections(): oldest = jax.lax.ppermute(oldest, GROUP, steps_seen)  190 us
    ppermute x15, waiting for transfers between devices, rows_times_shards(): lax.ppermute(sent, 'shard', pairs)  138 us
    ppermute x12, waiting for transfers between devices, scatter_product(): arrived.append(lax.ppermute(encode(chunk), 'shard', pairs))  136 us
    dot_general x36, matrix products, matmul(): jnp.dot(left_side, right_side, precision=lax.Precision.HIGH, preferred_el...  68.4 us
    dynamic_update_slice x24, local copies, waits for them, and re-layouts, plan_sections(): lax.dynamic_update_slice_in_dim(everything, long_array, (placed - ii) % k...  36.9 us
    ppermute x6, waiting for transfers between devices, shard_total(): total = total + lax.ppermute(tile, 'shard', pairs)[0, 0]  35.3 us
    dynamic_update_slice x18, local copies, waits for them, and re-layouts, plan_sections(): lax.dynamic_update_slice_in_dim(everything, oldest, (placed + ii) % kept_...  28.5 us
  transfers between devices with their start and end apart: 78, of which 59 were waited for; matrix products, arithmetic and copies ran while one was open for 12% of the time, Pallas kernels for 0%

profile of v1, /device:TPU:8, one launch (start us, length us, event | category | flops | bytes accessed | tf_op | source)
XLA Modules:
  0.0 1098.6 jit_solution(13016432669606429519)
XLA Ops:
  155.4 15.1 %collective-permute-done.15 = f32[640,320]{0,1:T(8,128)} collective-permute-done((f32[640,320]{0,1:T(8,128)}, f32[640,320]{0,1:T(8,128)}, u32[]{:S(2)}, u32[]{:S(2)}) %collective-permute-start.15) | collective-permute-done | bytes 819232 | tf_op jit(solution)/shard_map/ppermute | solution.py:37
  224.7 14.9 %collective-permute-done.19 = f32[640,320]{0,1:T(8,128)S(1)} collective-permute-done((f32[640,320]{0,1:T(8,128)}, f32[640,320]{0,1:T(8,128)S(1)}, u32[]{:S(2)}, u32[]{:S(2)}) %collective-permute-start.19) | collective-permute-done | bytes 819232 | tf_op jit(solution)/shard_map/ppermute | solution.py:37
  243.3 18.7 %collective-permute-done.26 = f32[640,320]{0,1:T(8,128)S(1)} collective-permute-done((f32[640,320]{0,1:T(8,128)S(1)}, f32[640,320]{0,1:T(8,128)S(1)}, u32[]{:S(2)}, u32[]{:S(2)}) %collective-permute-start.26) | collective-permute-done | bytes 819232 | tf_op jit(solution)/shard_map/ppermute | solution.py:37
  262.0 16.6 %collective-permute-done.27 = f32[640,320]{0,1:T(8,128)} collective-permute-done((f32[640,320]{0,1:T(8,128)S(1)}, f32[640,320]{0,1:T(8,128)}, u32[]{:S(2)}, u32[]{:S(2)}) %collective-permute-start.27) | collective-permute-done | bytes 819232 | tf_op jit(solution)/shard_map/ppermute | solution.py:42
  279.8 17.4 %collective-permute-done.28 = f32[640,320]{0,1:T(8,128)} collective-permute-done((f32[640,320]{0,1:T(8,128)S(1)}, f32[640,320]{0,1:T(8,128)}, u32[]{:S(2)}, u32[]{:S(2)}) %collective-permute-start.28) | collective-permute-done | bytes 819232 | tf_op jit(solution)/shard_map/ppermute | solution.py:37
  317.5 14.8 %collective-permute-done.30 = f32[640,320]{0,1:T(8,128)} collective-permute-done((f32[640,320]{0,1:T(8,128)}, f32[640,320]{0,1:T(8,128)}, u32[]{:S(2)}, u32[]{:S(2)}) %collective-permute-start.30) | collective-permute-done | bytes 819232 | tf_op jit(solution)/shard_map/ppermute | solution.py:37
  348.8 18.0 %collective-permute-done.32 = f32[640,320]{0,1:T(8,128)S(1)} collective-permute-done((f32[640,320]{0,1:T(8,128)}, f32[640,320]{0,1:T(8,128)S(1)}, u32[]{:S(2)}, u32[]{:S(2)}) %collective-permute-start.32) | collective-permute-done | bytes 819232 | tf_op jit(solution)/shard_map/ppermute | solution.py:37
  396.4 15.2 %collective-permute-done.20 = f32[640,320]{0,1:T(8,128)S(1)} collective-permute-done((f32[640,320]{0,1:T(8,128)S(1)}, f32[640,320]{0,1:T(8,128)S(1)}, u32[]{:S(2)}, u32[]{:S(2)}) %collective-permute-start.20) | collective-permute-done | bytes 819232 | tf_op jit(solution)/shard_map/ppermute | solution.py:119
  411.6 22.7 %collective-permute-done.21 = f32[640,320]{0,1:T(8,128)S(1)} collective-permute-done((f32[640,320]{0,1:T(8,128)S(1)}, f32[640,320]{0,1:T(8,128)S(1)}, u32[]{:S(2)}, u32[]{:S(2)}) %collective-permute-start.21) | collective-permute-done | bytes 819232 | tf_op jit(solution)/shard_map/ppermute | solution.py:119
  434.3 16.7 %collective-permute-done.22 = f32[640,320]{0,1:T(8,128)S(1)} collective-permute-done((f32[640,320]{0,1:T(8,128)S(1)}, f32[640,320]{0,1:T(8,128)S(1)}, u32[]{:S(2)}, u32[]{:S(2)}) %collective-permute-start.22) | collective-permute-done | bytes 819232 | tf_op jit(solution)/shard_map/ppermute | solution.py:119
  515.2 16.7 %collective-permute-done.42 = f32[640,320]{0,1:T(8,128)S(1)} collective-permute-done((f32[640,320]{0,1:T(8,128)S(1)}, f32[640,320]{0,1:T(8,128)S(1)}, u32[]{:S(2)}, u32[]{:S(2)}) %collective-permute-start.42) | collective-permute-done | bytes 819232 | tf_op jit(solution)/shard_map/ppermute | solution.py:37
  548.1 24.6 %collective-permute-done.43 = f32[8,128]{1,0:T(8,128)S(1)} collective-permute-done((f32[8,128]{1,0:T(8,128)S(1)}, f32[8,128]{1,0:T(8,128)S(1)}, u32[]{:S(2)}, u32[]{:S(2)}) %collective-permute-start.43) | collective-permute-done | bytes 4128 | tf_op jit(solution)/shard_map/ppermute | solution.py:89
  601.9 25.8 %collective-permute-done.50 = f16[656,320]{0,1:T(8,128)(2,1)S(1)} collective-permute-done((f16[656,320]{0,1:T(8,128)(2,1)S(1)}, f16[656,320]{0,1:T(8,128)(2,1)S(1)}, u32[]{:S(2)}, u32[]{:S(2)}) %collective-permute-start.50) | collective-permute-done | bytes 419872 | tf_op jit(solution)/shard_map/ppermute | solution.py:99
  647.5 18.6 %collective-permute-done.52 = f32[640,320]{0,1:T(8,128)S(1)} collective-permute-done((f32[640,320]{0,1:T(8,128)S(1)}, f32[640,320]{0,1:T(8,128)S(1)}, u32[]{:S(2)}, u32[]{:S(2)}) %collective-permute-start.52) | collective-permute-done | bytes 819232 | tf_op jit(solution)/shard_map/ppermute | solution.py:37
  668.5 15.5 %collective-permute-done.53 = f32[640,320]{0,1:T(8,128)S(1)} collective-permute-done((f32[640,320]{0,1:T(8,128)S(1)}, f32[640,320]{0,1:T(8,128)S(1)}, u32[]{:S(2)}, u32[]{:S(2)}) %collective-permute-start.53) | collective-permute-done | bytes 819232 | tf_op jit(solution)/shard_map/ppermute | solution.py:42
  686.4 14.8 %collective-permute-done.54 = f32[640,320]{0,1:T(8,128)S(1)} collective-permute-done((f32[640,320]{0,1:T(8,128)S(1)}, f32[640,320]{0,1:T(8,128)S(1)}, u32[]{:S(2)}, u32[]{:S(2)}) %collective-permute-start.54) | collective-permute-done | bytes 819232 | tf_op jit(solution)/shard_map/ppermute | solution.py:37
  703.7 15.5 %collective-permute-done.55 = f32[640,320]{0,1:T(8,128)S(1)} collective-permute-done((f32[640,320]{0,1:T(8,128)S(1)}, f32[640,320]{0,1:T(8,128)S(1)}, u32[]{:S(2)}, u32[]{:S(2)}) %collective-permute-start.55) | collective-permute-done | bytes 819232 | tf_op jit(solution)/shard_map/ppermute | solution.py:42
  721.5 14.8 %collective-permute-done.56 = f32[640,320]{0,1:T(8,128)S(1)} collective-permute-done((f32[640,320]{0,1:T(8,128)S(1)}, f32[640,320]{0,1:T(8,128)S(1)}, u32[]{:S(2)}, u32[]{:S(2)}) %collective-permute-start.56) | collective-permute-done | bytes 819232 | tf_op jit(solution)/shard_map/ppermute | solution.py:37
  739.3 15.0 %collective-permute-done.57 = f32[640,320]{0,1:T(8,128)S(1)} collective-permute-done((f32[640,320]{0,1:T(8,128)S(1)}, f32[640,320]{0,1:T(8,128)S(1)}, u32[]{:S(2)}, u32[]{:S(2)}) %collective-permute-start.57) | collective-permute-done | bytes 819232 | tf_op jit(solution)/shard_map/ppermute | solution.py:42
  754.3 17.1 %collective-permute-done.58 = f32[640,320]{0,1:T(8,128)S(1)} collective-permute-done((f32[640,320]{0,1:T(8,128)S(1)}, f32[640,320]{0,1:T(8,128)S(1)}, u32[]{:S(2)}, u32[]{:S(2)}) %collective-permute-start.58) | collective-permute-done | bytes 819232 | tf_op jit(solution)/shard_map/ppermute | solution.py:37
  780.9 14.6 %collective-permute-done.59 = f16[656,320]{0,1:T(8,128)(2,1)S(1)} collective-permute-done((f16[656,320]{0,1:T(8,128)(2,1)S(1)}, f16[656,320]{0,1:T(8,128)(2,1)S(1)}, u32[]{:S(2)}, u32[]{:S(2)}) %collective-permute-start.59) | collective-permute-done | bytes 419872 | tf_op jit(solution)/shard_map/ppermute | solution.py:119
  795.5 14.9 %collective-permute-done.60 = f16[656,320]{0,1:T(8,128)(2,1)S(1)} collective-permute-done((f16[656,320]{0,1:T(8,128)(2,1)S(1)}, f16[656,320]{0,1:T(8,128)(2,1)S(1)}, u32[]{:S(2)}, u32[]{:S(2)}) %collective-permute-start.60) | collective-permute-done | bytes 419872 | tf_op jit(solution)/shard_map/ppermute | solution.py:119
  829.0 14.8 %collective-permute-done.62 = f16[656,320]{0,1:T(8,128)(2,1)S(1)} collective-permute-done((f16[656,320]{0,1:T(8,128)(2,1)S(1)}, f16[656,320]{0,1:T(8,128)(2,1)S(1)}, u32[]{:S(2)}, u32[]{:S(2)}) %collective-permute-start.62) | collective-permute-done | bytes 419872 | tf_op jit(solution)/shard_map/ppermute | solution.py:99
  876.9 18.9 %collective-permute-done.65 = f32[640,320]{0,1:T(8,128)S(1)} collective-permute-done((f32[640,320]{0,1:T(8,128)S(1)}, f32[640,320]{0,1:T(8,128)S(1)}, u32[]{:S(2)}, u32[]{:S(2)}) %collective-permute-start.65) | collective-permute-done | bytes 819232 | tf_op jit(solution)/shard_map/ppermute | solution.py:37
  895.8 16.6 %collective-permute-done.66 = f32[640,320]{0,1:T(8,128)S(1)} collective-permute-done((f32[640,320]{0,1:T(8,128)S(1)}, f32[640,320]{0,1:T(8,128)S(1)}, u32[]{:S(2)}, u32[]{:S(2)}) %collective-permute-start.66) | collective-permute-done | bytes 819232 | tf_op jit(solution)/shard_map/ppermute | solution.py:42
  913.3 17.5 %collective-permute-done.67 = f32[640,320]{0,1:T(8,128)S(1)} collective-permute-done((f32[640,320]{0,1:T(8,128)S(1)}, f32[640,320]{0,1:T(8,128)S(1)}, u32[]{:S(2)}, u32[]{:S(2)}) %collective-permute-start.67) | collective-permute-done | bytes 819232 | tf_op jit(solution)/shard_map/ppermute | solution.py:37
  930.9 16.6 %collective-permute-done.68 = f32[640,320]{0,1:T(8,128)S(1)} collective-permute-done((f32[640,320]{0,1:T(8,128)S(1)}, f32[640,320]{0,1:T(8,128)S(1)}, u32[]{:S(2)}, u32[]{:S(2)}) %collective-permute-start.68) | collective-permute-done | bytes 819232 | tf_op jit(solution)/shard_map/ppermute | solution.py:42
  948.5 17.5 %collective-permute-done.69 = f32[640,320]{0,1:T(8,128)S(1)} collective-permute-done((f32[640,320]{0,1:T(8,128)S(1)}, f32[640,320]{0,1:T(8,128)S(1)}, u32[]{:S(2)}, u32[]{:S(2)}) %collective-permute-start.69) | collective-permute-done | bytes 819232 | tf_op jit(solution)/shard_map/ppermute | solution.py:37
  966.3 16.2 %collective-permute-done.70 = f32[640,320]{0,1:T(8,128)S(1)} collective-permute-done((f32[640,320]{0,1:T(8,128)S(1)}, f32[640,320]{0,1:T(8,128)S(1)}, u32[]{:S(2)}, u32[]{:S(2)}) %collective-permute-start.70) | collective-permute-done | bytes 819232 | tf_op jit(solution)/shard_map/ppermute | solution.py:42
  982.6 16.4 %collective-permute-done.71 = f32[640,320]{0,1:T(8,128)S(1)} collective-permute-done((f32[640,320]{0,1:T(8,128)S(1)}, f32[640,320]{0,1:T(8,128)S(1)}, u32[]{:S(2)}, u32[]{:S(2)}) %collective-permute-start.71) | collective-permute-done | bytes 819232 | tf_op jit(solution)/shard_map/ppermute | solution.py:37
  1020.9 17.6 %collective-permute-done.73 = f16[656,320]{0,1:T(8,128)(2,1)S(1)} collective-permute-done((f16[656,320]{0,1:T(8,128)(2,1)S(1)}, f16[656,320]{0,1:T(8,128)(2,1)S(1)}, u32[]{:S(2)}, u32[]{:S(2)}) %collective-permute-start.73) | collective-permute-done | bytes 419872 | tf_op jit(solution)/shard_map/ppermute | solution.py:119
  1068.2 16.9 %collective-permute-done.76 = f16[656,320]{0,1:T(8,128)(2,1)S(1)} collective-permute-done((f16[656,320]{0,1:T(8,128)(2,1)S(1)}, f16[656,320]{0,1:T(8,128)(2,1)S(1)}, u32[]{:S(2)}, u32[]{:S(2)}) %collective-permute-start.76) | collective-permute-done | bytes 419872 | tf_op jit(solution)/shard_map/ppermute | solution.py:99
  (352 shorter events, 543.1 us)
Async XLA Ops:
  49.6 50.7 %collective-permute-start.5 = (bf16[640,320]{1,0:T(8,128)(2,1)}, bf16[640,320]{1,0:T(8,128)(2,1)}, u32[]{:S(2)}, u32[]{:S(2)}) collective-permute-start(bf16[640,320]{1,0:T(8,128)(2,1)} %collective-permute-done.3), channel_id=1, source_target_pairs={{0,7},{1,0},{2,1},{3,2},{4,3},{5,4},{6,5},{7,6},{8,15},{9,8},{10,9... | collective-permute-start | bytes 1228808 | tf_op jit(solution)/shard_map/ppermute | solution.py:42
  59.4 48.0 %collective-permute-start.6 = (bf16[640,320]{1,0:T(8,128)(2,1)}, bf16[640,320]{1,0:T(8,128)(2,1)}, u32[]{:S(2)}, u32[]{:S(2)}) collective-permute-start(bf16[640,320]{1,0:T(8,128)(2,1)} %collective-permute-done.4), channel_id=1, source_target_pairs={{0,1},{1,2},{2,3},{3,4},{4,5},{5,6},{6,7},{7,0},{8,9},{9,10},{10,1... | collective-permute-start | bytes 1228808 | tf_op jit(solution)/shard_map/ppermute | solution.py:37
  116.7 37.0 %collective-permute-start.14 = (f32[640,320]{0,1:T(8,128)}, f32[640,320]{0,1:T(8,128)}, u32[]{:S(2)}, u32[]{:S(2)}) collective-permute-start(f32[640,320]{0,1:T(8,128)} %param.12), channel_id=1, source_target_pairs={{0,7},{1,0},{2,1},{3,2},{4,3},{5,4},{6,5},{7,6},{8,15},{9,8},{10,9... | collective-permute-start | bytes 2457608 | tf_op jit(solution)/shard_map/ppermute | solution.py:42
  135.4 35.1 %collective-permute-start.15 = (f32[640,320]{0,1:T(8,128)}, f32[640,320]{0,1:T(8,128)}, u32[]{:S(2)}, u32[]{:S(2)}) collective-permute-start(f32[640,320]{0,1:T(8,128)} %collective-permute-done.13), channel_id=1, source_target_pairs={{0,1},{1,2},{2,3},{3,4},{4,5},{5,6},{6,7},{7,0},{8,9},{9,10},{10,1... | collective-permute-start | bytes 2457608 | tf_op jit(solution)/shard_map/ppermute | solution.py:37
  137.6 70.2 %collective-permute-start.10 = (bf16[320,2560]{1,0:T(8,128)(2,1)}, bf16[320,2560]{1,0:T(8,128)(2,1)}, u32[]{:S(2)}, u32[]{:S(2)}) collective-permute-start(bf16[320,2560]{1,0:T(8,128)(2,1)} %constant_dynamic-slice_fusion), channel_id=1, source_target_pairs={{0,8},{1,9},{10,18},{11,19},{20,28},{21,29},{30,6},{31,7}} | collective-permute-start | bytes 4915208 | tf_op jit(solution)/shard_map/ppermute | solution.py:136
  138.9 68.9 %collective-permute-start.11 = (bf16[320,2560]{1,0:T(8,128)(2,1)}, bf16[320,2560]{1,0:T(8,128)(2,1)}, u32[]{:S(2)}, u32[]{:S(2)}) collective-permute-start(bf16[320,2560]{1,0:T(8,128)(2,1)} %constant_dynamic-slice_fusion), channel_id=1, source_target_pairs={{0,16},{1,17},{10,26},{11,27},{20,4},{21,5},{30,14},{31,15}} | collective-permute-start | bytes 4915208 | tf_op jit(solution)/shard_map/ppermute | solution.py:136
  140.8 67.0 %collective-permute-start.12 = (bf16[320,2560]{1,0:T(8,128)(2,1)}, bf16[320,2560]{1,0:T(8,128)(2,1)}, u32[]{:S(2)}, u32[]{:S(2)}) collective-permute-start(bf16[320,2560]{1,0:T(8,128)(2,1)} %constant_dynamic-slice_fusion), channel_id=1, source_target_pairs={{0,24},{1,25},{10,2},{11,3},{20,12},{21,13},{30,22},{31,23}} | collective-permute-start | bytes 4915208 | tf_op jit(solution)/shard_map/ppermute | solution.py:136
  153.7 35.1 %collective-permute-start.16 = (f32[640,320]{0,1:T(8,128)}, f32[640,320]{0,1:T(8,128)}, u32[]{:S(2)}, u32[]{:S(2)}) collective-permute-start(f32[640,320]{0,1:T(8,128)} %collective-permute-done.14), channel_id=1, source_target_pairs={{0,7},{1,0},{2,1},{3,2},{4,3},{5,4},{6,5},{7,6},{8,15},{9,8},{10,9... | collective-permute-start | bytes 2457608 | tf_op jit(solution)/shard_map/ppermute | solution.py:42
  170.5 35.1 %collective-permute-start.17 = (f32[640,320]{0,1:T(8,128)}, f32[640,320]{0,1:T(8,128)}, u32[]{:S(2)}, u32[]{:S(2)}) collective-permute-start(f32[640,320]{0,1:T(8,128)} %collective-permute-done.15), channel_id=1, source_target_pairs={{0,1},{1,2},{2,3},{3,4},{4,5},{5,6},{6,7},{7,0},{8,9},{9,10},{10,1... | collective-permute-start | bytes 2457608 | tf_op jit(solution)/shard_map/ppermute | solution.py:37
  240.6 38.0 %collective-permute-start.27 = (f32[640,320]{0,1:T(8,128)S(1)}, f32[640,320]{0,1:T(8,128)}, u32[]{:S(2)}, u32[]{:S(2)}) collective-permute-start(f32[640,320]{0,1:T(8,128)S(1)} %fusion.188), channel_id=1, source_target_pairs={{0,7},{1,0},{2,1},{3,2},{4,3},{5,4},{6,5},{7,6},{8,15},{9,8},{10,9... | collective-permute-start | bytes 2457608 | tf_op jit(solution)/shard_map/ppermute | solution.py:42
  262.0 35.2 %collective-permute-start.28 = (f32[640,320]{0,1:T(8,128)S(1)}, f32[640,320]{0,1:T(8,128)}, u32[]{:S(2)}, u32[]{:S(2)}) collective-permute-start(f32[640,320]{0,1:T(8,128)S(1)} %collective-permute-done.26), channel_id=1, source_target_pairs={{0,1},{1,2},{2,3},{3,4},{4,5},{5,6},{6,7},{7,0},{8,9},{9,10},{10,1... | collective-permute-start | bytes 2457608 | tf_op jit(solution)/shard_map/ppermute | solution.py:37
  297.4 69.4 %collective-permute-start.34 = (f32[640,320]{0,1:T(8,128)}, f32[640,320]{0,1:T(8,128)S(1)}, u32[]{:S(2)}, u32[]{:S(2)}) collective-permute-start(f32[640,320]{0,1:T(8,128)} %param.12), channel_id=1, source_target_pairs={{0,16},{8,24},{16,0},{24,8},{1,17},{9,25},{17,1},{25,9},{2,18},{10... | collective-permute-start | bytes 2457608 | tf_op jit(solution)/shard_map/ppermute | solution.py:99
  300.0 68.1 %collective-permute-start.33 = (f32[640,320]{0,1:T(8,128)}, f32[640,320]{0,1:T(8,128)}, u32[]{:S(2)}, u32[]{:S(2)}) collective-permute-start(f32[640,320]{0,1:T(8,128)} %param.12), channel_id=1, source_target_pairs={{0,8},{8,0},{16,24},{24,16},{1,9},{9,1},{17,25},{25,17},{2,10},{10... | collective-permute-start | bytes 2457608 | tf_op jit(solution)/shard_map/ppermute | solution.py:99
  300.5 70.1 %collective-permute-start.35 = (f32[640,320]{0,1:T(8,128)}, f32[640,320]{0,1:T(8,128)S(1)}, u32[]{:S(2)}, u32[]{:S(2)}) collective-permute-start(f32[640,320]{0,1:T(8,128)} %param.12), channel_id=1, source_target_pairs={{0,24},{8,16},{16,8},{24,0},{1,25},{9,17},{17,9},{25,1},{2,26},{10... | collective-permute-start | bytes 2457608 | tf_op jit(solution)/shard_map/ppermute | solution.py:99
  377.6 56.6 %collective-permute-start.21 = (f32[640,320]{0,1:T(8,128)S(1)}, f32[640,320]{0,1:T(8,128)S(1)}, u32[]{:S(2)}, u32[]{:S(2)}) collective-permute-start(f32[640,320]{0,1:T(8,128)S(1)} %fusion.67), channel_id=1, source_target_pairs={{0,16},{8,24},{16,0},{24,8},{1,17},{9,25},{17,1},{25,9},{2,18},{10... | collective-permute-start | bytes 2457608 | tf_op jit(solution)/shard_map/ppermute | solution.py:119
  380.5 70.5 %collective-permute-start.22 = (f32[640,320]{0,1:T(8,128)S(1)}, f32[640,320]{0,1:T(8,128)S(1)}, u32[]{:S(2)}, u32[]{:S(2)}) collective-permute-start(f32[640,320]{0,1:T(8,128)S(1)} %fusion.63), channel_id=1, source_target_pairs={{0,24},{8,16},{16,8},{24,0},{1,25},{9,17},{17,9},{25,1},{2,26},{10... | collective-permute-start | bytes 2457608 | tf_op jit(solution)/shard_map/ppermute | solution.py:119
  380.9 76.3 %collective-permute-start.37 = (f32[640,320]{0,1:T(8,128)S(1)}, f32[640,320]{0,1:T(8,128)S(1)}, u32[]{:S(2)}, u32[]{:S(2)}) collective-permute-start(f32[640,320]{0,1:T(8,128)S(1)} %get-tuple-element.51), channel_id=1, source_target_pairs={{0,7},{1,0},{2,1},{3,2},{4,3},{5,4},{6,5},{7,6},{8,15},{9,8},{10,9... | collective-permute-start | bytes 2457608 | tf_op jit(solution)/shard_map/ppermute | solution.py:42
  396.4 62.3 %collective-permute-start.38 = (f32[640,320]{0,1:T(8,128)S(1)}, f32[640,320]{0,1:T(8,128)S(1)}, u32[]{:S(2)}, u32[]{:S(2)}) collective-permute-start(f32[640,320]{0,1:T(8,128)S(1)} %collective-permute-done.36), channel_id=1, source_target_pairs={{0,1},{1,2},{2,3},{3,4},{4,5},{5,6},{6,7},{7,0},{8,9},{9,10},{10,1... | collective-permute-start | bytes 2457608 | tf_op jit(solution)/shard_map/ppermute | solution.py:37
  457.2 36.7 %collective-permute-start.39 = (f32[640,320]{0,1:T(8,128)S(1)}, f32[640,320]{0,1:T(8,128)S(1)}, u32[]{:S(2)}, u32[]{:S(2)}) collective-permute-start(f32[640,320]{0,1:T(8,128)S(1)} %collective-permute-done.37), channel_id=1, source_target_pairs={{0,7},{1,0},{2,1},{3,2},{4,3},{5,4},{6,5},{7,6},{8,15},{9,8},{10,9... | collective-permute-start | bytes 2457608 | tf_op jit(solution)/shard_map/ppermute | solution.py:42
  458.7 38.3 %collective-permute-start.40 = (f32[640,320]{0,1:T(8,128)S(1)}, f32[640,320]{0,1:T(8,128)S(1)}, u32[]{:S(2)}, u32[]{:S(2)}) collective-permute-start(f32[640,320]{0,1:T(8,128)S(1)} %collective-permute-done.38), channel_id=1, source_target_pairs={{0,1},{1,2},{2,3},{3,4},{4,5},{5,6},{6,7},{7,0},{8,9},{9,10},{10,1... | collective-permute-start | bytes 2457608 | tf_op jit(solution)/shard_map/ppermute | solution.py:37
  537.6 50.0 %collective-permute-start.46 = (f16[656,320]{0,1:T(8,128)(2,1)}, f16[656,320]{0,1:T(8,128)(2,1)}, u32[]{:S(2)}, u32[]{:S(2)}) collective-permute-start(f16[656,320]{0,1:T(8,128)(2,1)} %pad_maximum_fusion), channel_id=1, source_target_pairs={{0,8},{8,0},{16,24},{24,16},{1,9},{9,1},{17,25},{25,17},{2,10},{10... | collective-permute-start | bytes 1259528 | tf_op jit(solution)/shard_map/ppermute | solution.py:119
  538.8 49.9 %collective-permute-start.47 = (f16[656,320]{0,1:T(8,128)(2,1)}, f16[656,320]{0,1:T(8,128)(2,1)}, u32[]{:S(2)}, u32[]{:S(2)}) collective-permute-start(f16[656,320]{0,1:T(8,128)(2,1)} %pad_maximum_fusion.1), channel_id=1, source_target_pairs={{0,16},{8,24},{16,0},{24,8},{1,17},{9,25},{17,1},{25,9},{2,18},{10... | collective-permute-start | bytes 1259528 | tf_op jit(solution)/shard_map/ppermute | solution.py:119
  541.0 49.1 %collective-permute-start.48 = (f16[656,320]{0,1:T(8,128)(2,1)}, f16[656,320]{0,1:T(8,128)(2,1)}, u32[]{:S(2)}, u32[]{:S(2)}) collective-permute-start(f16[656,320]{0,1:T(8,128)(2,1)} %pad_maximum_fusion.2), channel_id=1, source_target_pairs={{0,24},{8,16},{16,8},{24,0},{1,25},{9,17},{17,9},{25,1},{2,26},{10... | collective-permute-start | bytes 1259528 | tf_op jit(solution)/shard_map/ppermute | solution.py:119
  595.9 45.2 %collective-permute-start.51 = (f16[656,320]{0,1:T(8,128)(2,1)S(1)}, f16[656,320]{0,1:T(8,128)(2,1)S(1)}, u32[]{:S(2)}, u32[]{:S(2)}) collective-permute-start(f16[656,320]{0,1:T(8,128)(2,1)S(1)} %pad_maximum_fusion.3), channel_id=1, source_target_pairs={{0,24},{8,16},{16,8},{24,0},{1,25},{9,17},{17,9},{25,1},{2,26},{10... | collective-permute-start | bytes 1259528 | tf_op jit(solution)/shard_map/ppermute | solution.py:99
  599.8 42.9 %collective-permute-start.49 = (f16[656,320]{0,1:T(8,128)(2,1)S(1)}, f16[656,320]{0,1:T(8,128)(2,1)S(1)}, u32[]{:S(2)}, u32[]{:S(2)}) collective-permute-start(f16[656,320]{0,1:T(8,128)(2,1)S(1)} %pad_maximum_fusion.3), channel_id=1, source_target_pairs={{0,8},{8,0},{16,24},{24,16},{1,9},{9,1},{17,25},{25,17},{2,10},{10... | collective-permute-start | bytes 1259528 | tf_op jit(solution)/shard_map/ppermute | solution.py:99
  647.4 36.6 %collective-permute-start.53 = (f32[640,320]{0,1:T(8,128)S(1)}, f32[640,320]{0,1:T(8,128)S(1)}, u32[]{:S(2)}, u32[]{:S(2)}) collective-permute-start(f32[640,320]{0,1:T(8,128)S(1)} %get-tuple-element.61), channel_id=1, source_target_pairs={{0,7},{1,0},{2,1},{3,2},{4,3},{5,4},{6,5},{7,6},{8,15},{9,8},{10,9... | collective-permute-start | bytes 2457608 | tf_op jit(solution)/shard_map/ppermute | solution.py:42
  684.0 35.1 %collective-permute-start.55 = (f32[640,320]{0,1:T(8,128)S(1)}, f32[640,320]{0,1:T(8,128)S(1)}, u32[]{:S(2)}, u32[]{:S(2)}) collective-permute-start(f32[640,320]{0,1:T(8,128)S(1)} %collective-permute-done.53), channel_id=1, source_target_pairs={{0,7},{1,0},{2,1},{3,2},{4,3},{5,4},{6,5},{7,6},{8,15},{9,8},{10,9... | collective-permute-start | bytes 2457608 | tf_op jit(solution)/shard_map/ppermute | solution.py:42
  778.4 44.6 %collective-permute-start.61 = (f16[656,320]{0,1:T(8,128)(2,1)S(1)}, f16[656,320]{0,1:T(8,128)(2,1)S(1)}, u32[]{:S(2)}, u32[]{:S(2)}) collective-permute-start(f16[656,320]{0,1:T(8,128)(2,1)S(1)} %pad_maximum_fusion.6), channel_id=1, source_target_pairs={{0,24},{8,16},{16,8},{24,0},{1,25},{9,17},{17,9},{25,1},{2,26},{10... | collective-permute-start | bytes 1259528 | tf_op jit(solution)/shard_map/ppermute | solution.py:119
  826.6 43.9 %collective-permute-start.64 = (f16[656,320]{0,1:T(8,128)(2,1)S(1)}, f16[656,320]{0,1:T(8,128)(2,1)S(1)}, u32[]{:S(2)}, u32[]{:S(2)}) collective-permute-start(f16[656,320]{0,1:T(8,128)(2,1)S(1)} %pad_maximum_fusion.7), channel_id=1, source_target_pairs={{0,24},{8,16},{16,8},{24,0},{1,25},{9,17},{17,9},{25,1},{2,26},{10... | collective-permute-start | bytes 1259528 | tf_op jit(solution)/shard_map/ppermute | solution.py:99
  874.3 38.1 %collective-permute-start.66 = (f32[640,320]{0,1:T(8,128)S(1)}, f32[640,320]{0,1:T(8,128)S(1)}, u32[]{:S(2)}, u32[]{:S(2)}) collective-permute-start(f32[640,320]{0,1:T(8,128)S(1)} %get-tuple-element.71), channel_id=1, source_target_pairs={{0,7},{1,0},{2,1},{3,2},{4,3},{5,4},{6,5},{7,6},{8,15},{9,8},{10,9... | collective-permute-start | bytes 2457608 | tf_op jit(solution)/shard_map/ppermute | solution.py:42
  1006.2 42.4 %collective-permute-start.74 = (f16[656,320]{0,1:T(8,128)(2,1)S(1)}, f16[656,320]{0,1:T(8,128)(2,1)S(1)}, u32[]{:S(2)}, u32[]{:S(2)}) collective-permute-start(f16[656,320]{0,1:T(8,128)(2,1)S(1)} %pad_maximum_fusion.10), channel_id=1, source_target_pairs={{0,24},{8,16},{16,8},{24,0},{1,25},{9,17},{17,9},{25,1},{2,26},{10... | collective-permute-start | bytes 1259528 | tf_op jit(solution)/shard_map/ppermute | solution.py:119
  1053.1 41.0 %collective-permute-start.77 = (f16[656,320]{0,1:T(8,128)(2,1)S(1)}, f16[656,320]{0,1:T(8,128)(2,1)S(1)}, u32[]{:S(2)}, u32[]{:S(2)}) collective-permute-start(f16[656,320]{0,1:T(8,128)(2,1)S(1)} %pad_maximum_fusion.11), channel_id=1, source_target_pairs={{0,24},{8,16},{16,8},{24,0},{1,25},{9,17},{17,9},{25,1},{2,26},{10... | collective-permute-start | bytes 1259528 | tf_op jit(solution)/shard_map/ppermute | solution.py:99
  (65 other events, 2166.4 us)
